TPU v7x, 128 devices: a whole 4x4x4 slice. The times are simulated.
128 devices in a mesh: pairs: 32 (over y, z, core), items: 4 (over x).
Axes of the slice: x: 4, y: 4, z: 4, core: 2. Of those that a mesh axis runs over, the one named last changes fastest.
Arguments:
- user_table: bfloat16 [131072, 1024], P(('pairs', 'items'))
- item_table: bfloat16 [8192, 1024], P('items')
- pair_user: int32 [262144], P(('pairs', 'items')), may hold values from 0 to 1023
- pair_item: int32 [262144], P(('pairs', 'items')), may hold values from 0 to 2047
- pair_owner: int32 [262144], P(('pairs', 'items')), may hold values from 0 to 3, as said below
- pair_count: int32 [128], P(('pairs', 'items')), may hold values from 1024 to 2048, as said below
Outputs:
- r_user: float32 [1024, 1024], replicated
- r_item: float32 [1024, 1024], replicated
- whitened: float32 [1024, 1024], P(('pairs', 'items'))
Inputs may be any that keep to these rules, and one draw needn't show every extreme that they name: `pair_owner`: among the 2048 pair slots of one device at most 1024 name one owner; in every group of devices along items one owner is named by exactly 1024 slots of every device of the group. `pair_count`: some device has all 2048 slots valid.
All inputs are finite; a program needn't handle non-finite values.
Results may differ from a plain program's by a relative error of at most 0.0003.
Values may be sent and summed in bfloat16 or wider, within the bound.
No kernel may reach another device: no remote copies, remote signals or barrier semaphores. Data moves between devices by JAX's collectives and lax.ppermute only.
A program may use at most 128 MiB of HBM per device.

v0:
```python
import jax
import jax.numpy as jnp
from jax import lax
from jax.sharding import PartitionSpec as P


def body(user_table, item_table, pair_user, pair_item, pair_owner, pair_count):
    owners = lax.axis_size("items")
    devices = lax.axis_size("pairs") * owners
    slots_dev = pair_owner.shape[0]
    width = user_table.shape[1]
    total = float(slots_dev * devices)
    capacity = slots_dev // 2
    onehot = (pair_owner[:, None] == jnp.arange(owners, dtype=jnp.int32)[None, :]).astype(jnp.int32)
    ranks = jnp.sum(onehot * (jnp.cumsum(onehot, axis=0) - 1), axis=1)
    flat_slot = pair_owner * capacity + ranks
    request = jnp.zeros((owners * capacity,), jnp.int32).at[flat_slot].set(pair_item)
    request = request.reshape(owners, capacity)
    wanted = lax.all_to_all(request, "items", split_axis=0, concat_axis=0, tiled=True)
    rows = jnp.take(item_table, wanted.reshape(-1), axis=0)
    rows = rows.reshape(wanted.shape[0], wanted.shape[1], width)
    fetched = lax.all_to_all(rows, "items", split_axis=0, concat_axis=0, tiled=True)
    item_raw = jnp.take(fetched.reshape(owners * capacity, width), flat_slot, axis=0)
    keep = (jnp.arange(slots_dev, dtype=jnp.int32) < pair_count[0])[:, None]
    user_raw = jnp.take(user_table, pair_user, axis=0)
    user_panel = jnp.where(keep, user_raw, jnp.zeros((), jnp.bfloat16))
    item_panel = jnp.where(keep, item_raw, jnp.zeros((), jnp.bfloat16))
    dims = (((0,), (0,)), ((), ()))
    gram_user = lax.dot_general(user_panel, user_panel, dims, preferred_element_type=jnp.float32)
    gram_item = lax.dot_general(item_panel, item_panel, dims, preferred_element_type=jnp.float32)
    cross = lax.dot_general(user_panel, item_panel, dims, preferred_element_type=jnp.float32)
    rows_out = width // devices
    root_total = jnp.sqrt(jnp.float32(total))
    gram_user, gram_item, cross = lax.psum((gram_user, gram_item, cross), ("pairs", "items"))
    lower_user = jnp.linalg.cholesky(gram_user / total)
    lower_item = jnp.linalg.cholesky(gram_item / total)
    left = jax.scipy.linalg.solve_triangular(lower_user, cross / total, lower=True)
    full = jax.scipy.linalg.solve_triangular(lower_item, left.T, lower=True).T * root_total
    position = lax.axis_index(("pairs", "items"))
    whitened = lax.dynamic_slice_in_dim(full, position * rows_out, rows_out, 0)
    return (lower_user.T, lower_item.T, whitened)


def solution(mesh):
    placed = (
        P(("pairs", "items"), None),
        P("items", None),
        P(("pairs", "items")),
        P(("pairs", "items")),
        P(("pairs", "items")),
        P(("pairs", "items")),
    )
    return jax.shard_map(
        body,
        mesh=mesh,
        in_specs=placed,
        out_specs=(P(), P(), P(("pairs", "items"), None)),
        check_vma=False,
    )
```

profile of v0, /device:TPU:1, one launch (start us, length us, event | category | flops | bytes accessed | tf_op | source)
XLA Modules:
  0.0 1121.6 jit_solution(1224190746724436281)
XLA Ops:
  28.2 23.6 %gather_fusion.1 = bf16[4096,1024]{1,0:T(8,128)(2,1)} fusion(bf16[2048,1024]{1,0:T(8,128)(2,1)} %param.10, s32[4096]{0:T(1024)S(1)} %broadcast_clamp_fusion), kind=kCustom, calls=%fused_computation.1 | custom fusion | bytes 16793600 | tf_op jit(solution)/shard_map/jit(_take)/gather | solution.py:20
  75.3 10.5 fusion.150
  85.8 71.0 %all-to-all-done.1 = bf16[4,1024,1024]{2,1,0:T(8,128)(2,1)} async-done(((bf16[4,1024,1024]{2,1,0:T(8,128)(2,1)}), bf16[4,1024,1024]{2,1,0:T(8,128)(2,1)}, u32[]{:S(2)}, u32[]{:S(2)}) %all-to-all-start.1) | async-done | bytes 8388640 | tf_op jit(solution)/shard_map/all_to_all | solution.py:22
  156.7 15.7 %gather_fusion.2 = bf16[2048,1024]{1,0:T(8,128)(2,1)} fusion(bf16[4096,1024]{1,0:T(8,128)(2,1)} %bitcast.23, s32[2048]{0:T(1024)S(1)} %broadcast_clamp_fusion.1), kind=kCustom, calls=%fused_computation.2 | custom fusion | bytes 8396800 | tf_op jit(solution)/shard_map/jit(_take)/gather | solution.py:23
  172.4 10.5 fusion.149
  190.0 173.9 %all-reduce.4.cloned.1.call-done = (f32[1024,1024]{0,1:T(8,128)}, f32[1024,1024]{0,1:T(8,128)}, f32[1024,1024]{0,1:T(8,128)}) async-done(((f32[1024,1024]{0,1:T(8,128)}, f32[1024,1024]{0,1:T(8,128)}, f32[1024,1024]{0,1:T(8,128)}), (f32[1024,1024]{0,1:T(8,128)}, f32[1024,1024]{0,1:T(8,128)}, f32[1024,1024]{0,1:T(8,128)})) %all-reduce.4.cloned.1.call-update) | async-done | bytes 12582928 | tf_op jit(solution)/shard_map/psum | solution.py:34
  381.1 11.7 %cholesky.619 = f32[128,128]{1,0:T(8,128)S(1)} custom-call(f32[128,128]{1,0:T(8,128)S(1)} %cholesky.911), custom_call_target="Cholesky" | custom-call | tf_op jit(solution)/shard_map/jit(cholesky)/cholesky | solution.py:35
  392.9 9.8 custom-call.55
  409.1 11.9 %cholesky.638 = f32[128,128]{1,0:T(8,128)S(1)} custom-call(f32[128,128]{1,0:T(8,128)S(1)} %cholesky.915), custom_call_target="Cholesky" | custom-call | tf_op jit(solution)/shard_map/jit(cholesky)/cholesky | solution.py:35
  436.1 11.7 %cholesky.659 = f32[128,128]{1,0:T(8,128)S(1)} custom-call(f32[128,128]{1,0:T(8,128)S(1)} %cholesky.920), custom_call_target="Cholesky" | custom-call | tf_op jit(solution)/shard_map/jit(cholesky)/cholesky | solution.py:35
  449.1 9.8 custom-call.57
  462.4 11.9 %cholesky.678 = f32[128,128]{1,0:T(8,128)S(1)} custom-call(f32[128,128]{1,0:T(8,128)S(1)} %cholesky.925), custom_call_target="Cholesky" | custom-call | tf_op jit(solution)/shard_map/jit(cholesky)/cholesky | solution.py:35
  488.8 11.7 %cholesky.697 = f32[128,128]{1,0:T(8,128)S(1)} custom-call(f32[128,128]{1,0:T(8,128)S(1)} %cholesky.930), custom_call_target="Cholesky" | custom-call | tf_op jit(solution)/shard_map/jit(cholesky)/cholesky | solution.py:35
  501.9 10.2 custom-call.59
  515.4 11.7 %cholesky.716 = f32[128,128]{1,0:T(8,128)S(1)} custom-call(f32[128,128]{1,0:T(8,128)S(1)} %cholesky.935), custom_call_target="Cholesky" | custom-call | tf_op jit(solution)/shard_map/jit(cholesky)/cholesky | solution.py:35
  541.2 11.9 %cholesky.735 = f32[128,128]{1,0:T(8,128)S(1)} custom-call(f32[128,128]{1,0:T(8,128)S(1)} %cholesky.940), custom_call_target="Cholesky" | custom-call | tf_op jit(solution)/shard_map/jit(cholesky)/cholesky | solution.py:35
  566.9 11.7 %cholesky.752 = f32[128,128]{1,0:T(8,128)S(1)} custom-call(f32[128,128]{1,0:T(8,128)S(1)} %convolution_subtract_fusion.23), custom_call_target="Cholesky" | custom-call | tf_op jit(solution)/shard_map/jit(cholesky)/cholesky | solution.py:35
  591.8 23.2 %while.4 = (s32[]{:T(128)}, f32[1024,1024]{1,0:T(8,128)}, s32[8,2]{0,1:T(2,128)S(1)}, f32[8,128,128]{2,1,0:T(8,128)S(1)}, s32[]{:T(128)}) while((s32[]{:T(128)}, f32[1024,1024]{1,0:T(8,128)}, s32[8,2]{0,1:T(2,128)S(1)}, f32[8,128,128]{2,1,0:T(8,128)S(1)}, s32[]{:T(128)}) %tuple.121), condition=%wide.while_cond, body=%wide.while_body.sunk | while | flops 2 | bytes 131181 | solution.py:37
  615.0 78.8 %custom-call.69 = f32[8,128,128]{1,2,0:T(8,128)S(1)} custom-call(f32[8,128,128]{2,1,0:T(8,128)S(1)} %get-tuple-element.19), custom_call_target="InvertDiagBlocksLowerTriangular" | custom-call | tf_op jit(solution)/shard_map/jit(_solve_triangular)/triangular_solve | solution.py:37
  749.4 11.7 %cholesky.767 = f32[128,128]{1,0:T(8,128)S(1)} custom-call(f32[128,128]{1,0:T(8,128)S(1)} %cholesky.944), custom_call_target="Cholesky" | custom-call | tf_op jit(solution)/shard_map/jit(cholesky)/cholesky | solution.py:36
  761.1 9.8 custom-call.62
  777.4 12.1 %cholesky.786 = f32[128,128]{1,0:T(8,128)S(1)} custom-call(f32[128,128]{1,0:T(8,128)S(1)} %cholesky.948), custom_call_target="Cholesky" | custom-call | tf_op jit(solution)/shard_map/jit(cholesky)/cholesky | solution.py:36
  804.5 11.7 %cholesky.807 = f32[128,128]{1,0:T(8,128)S(1)} custom-call(f32[128,128]{1,0:T(8,128)S(1)} %cholesky.953), custom_call_target="Cholesky" | custom-call | tf_op jit(solution)/shard_map/jit(cholesky)/cholesky | solution.py:36
  817.5 9.8 custom-call.64
  830.8 11.9 %cholesky.826 = f32[128,128]{1,0:T(8,128)S(1)} custom-call(f32[128,128]{1,0:T(8,128)S(1)} %cholesky.958), custom_call_target="Cholesky" | custom-call | tf_op jit(solution)/shard_map/jit(cholesky)/cholesky | solution.py:36
  857.3 11.7 %cholesky.845 = f32[128,128]{1,0:T(8,128)S(1)} custom-call(f32[128,128]{1,0:T(8,128)S(1)} %cholesky.963), custom_call_target="Cholesky" | custom-call | tf_op jit(solution)/shard_map/jit(cholesky)/cholesky | solution.py:36
  870.3 10.0 custom-call.66
  883.6 11.7 %cholesky.864 = f32[128,128]{1,0:T(8,128)S(1)} custom-call(f32[128,128]{1,0:T(8,128)S(1)} %cholesky.968), custom_call_target="Cholesky" | custom-call | tf_op jit(solution)/shard_map/jit(cholesky)/cholesky | solution.py:36
  909.4 12.1 %cholesky.883 = f32[128,128]{1,0:T(8,128)S(1)} custom-call(f32[128,128]{1,0:T(8,128)S(1)} %cholesky.973), custom_call_target="Cholesky" | custom-call | tf_op jit(solution)/shard_map/jit(cholesky)/cholesky | solution.py:36
  935.4 11.7 %cholesky.900 = f32[128,128]{1,0:T(8,128)S(1)} custom-call(f32[128,128]{1,0:T(8,128)S(1)} %convolution_subtract_fusion.22), custom_call_target="Cholesky" | custom-call | tf_op jit(solution)/shard_map/jit(cholesky)/cholesky | solution.py:36
  960.2 23.0 %while.5 = (s32[]{:T(128)}, f32[1024,1024]{1,0:T(8,128)}, s32[8,2]{0,1:T(2,128)S(1)}, f32[8,128,128]{2,1,0:T(8,128)S(1)}, s32[]{:T(128)}) while((s32[]{:T(128)}, f32[1024,1024]{1,0:T(8,128)}, s32[8,2]{0,1:T(2,128)S(1)}, f32[8,128,128]{2,1,0:T(8,128)S(1)}, s32[]{:T(128)}) %tuple.130), condition=%wide.while_cond.clone, body=%wide.while_body.clone.sunk | while | flops 2 | bytes 131181 | solution.py:38
  983.2 78.8 %custom-call.70 = f32[8,128,128]{1,2,0:T(8,128)S(1)} custom-call(f32[8,128,128]{2,1,0:T(8,128)S(1)} %get-tuple-element.20), custom_call_target="InvertDiagBlocksLowerTriangular" | custom-call | tf_op jit(solution)/shard_map/jit(_solve_triangular)/triangular_solve | solution.py:38
  (218 shorter events, 384.5 us)
Async XLA Ops:
  7.2 58.5 %copy-start = (bf16[1024,1024]{1,0:T(8,128)(2,1)S(1)}, bf16[1024,1024]{1,0:T(8,128)(2,1)}, u32[]{:S(2)}) copy-start(bf16[1024,1024]{1,0:T(8,128)(2,1)} %param.9) | copy-start | bytes 6291460
  59.1 6.5 copy-start.8
  59.1 97.6 %all-to-all-start.1 = ((bf16[4,1024,1024]{2,1,0:T(8,128)(2,1)}), bf16[4,1024,1024]{2,1,0:T(8,128)(2,1)}, u32[]{:S(2)}, u32[]{:S(2)}) async-start(bf16[4,1024,1024]{2,1,0:T(8,128)(2,1)} %broadcast_select_fusion), calls=%async_computation.1 | async-start | bytes 16777216 | tf_op jit(solution)/shard_map/all_to_all | solution.py:22
  64.9 298.9 %all-reduce.4.cloned.1.call-start = ((), (), s32[]{:S(2)}) async-start(), calls=%async_computation.2 | async-start | bytes 25165824 | tf_op jit(solution)/shard_map/psum | solution.py:34
  172.4 10.5 copy-start.5
  379.1 2.0 copy-start.3
  725.5 9.6 copy-start.2
  726.2 8.9 copy-start.6
  747.4 2.0 copy-start.4
  1063.5 4.8 copy-start.7
  1108.9 5.5 copy-start.1
Sparse Core Ops, SparseCore 0:
  190.1 173.7 all-reduce.3
where the time goes:
time: 1130 us; the launch traced here: 1120 us
  other arithmetic  548 us (48%)
  waiting for transfers between devices  245 us (22%)
  matrix products  153 us (14%)
  local copies, waits for them, and re-layouts  135 us (12%)
  between operations  25.9 us (2%)
    psum x1, waiting for transfers between devices, body(): lax.psum((gram_user, gram_item, cross), ('pairs', 'items'))  174 us
    another operation x31, other arithmetic, body(): lower_item = jnp.linalg.cholesky(gram_item / total)  173 us
    another operation x31, other arithmetic, body(): lower_user = jnp.linalg.cholesky(gram_user / total)  173 us
    another operation x2, other arithmetic, body(): jax.scipy.linalg.solve_triangular(lower_user, cross / total, lower=True)  85.6 us
    another operation x3, other arithmetic, body(): jax.scipy.linalg.solve_triangular(lower_item, left.T, lower=True)  85.6 us
    all_to_all x1, waiting for transfers between devices, body(): lax.all_to_all(rows, 'items', split_axis=0, concat_axis=0, tiled=True)  71 us
    another operation x15, matrix products, body(): jax.scipy.linalg.solve_triangular(lower_user, cross / total, lower=True)  40 us
    another operation x15, matrix products, body(): jax.scipy.linalg.solve_triangular(lower_item, left.T, lower=True)  38.9 us
  transfers between devices with their start and end apart: 2, of which 2 were waited for; matrix products, arithmetic and copies ran while one was open for 2% of the time, Pallas kernels for 0%

commit v1 on v0

--- a/solution.py
+++ b/solution.py
@@ -1,7 +1,172 @@
 import jax
 import jax.numpy as jnp
 from jax import lax
+from jax.experimental import pallas as pl
+from jax.experimental.pallas import tpu as pltpu
 from jax.sharding import PartitionSpec as P
+
+N = 1024
+NB = 128
+KB = N // NB
+SUB = 32
+HI = lax.Precision.HIGHEST
+F32 = jnp.float32
+
+
+def row_of(v, t):
+    return jnp.broadcast_to(v[t:t + 1, :], v.shape)
+
+
+def lane_of(v, c):
+    return jnp.broadcast_to(v[:, c:c + 1], (8, NB))
+
+
+def dot(a, b, ca, cb):
+    return lax.dot_general(a, b, (((ca,), (cb,)), ((), ())), precision=HI, preferred_element_type=F32)
+
+
+def factor(refs):
+    sub = lax.broadcasted_iota(jnp.int32, (8, NB), 0)
+    groups = SUB // 8
+    for s in range(NB // SUB):
+        panels = [[(r[SUB * s + 8 * g:SUB * s + 8 * g + 8, :NB], r[SUB * s + 8 * g:SUB * s + 8 * g + 8, NB:]) for g in range(groups)] for r in refs]
+        for g in range(groups):
+            for m, r in enumerate(refs):
+                base = SUB * s + 8 * g
+                left, right = panels[m][g]
+                cols = [lane_of(left, base + t) for t in range(8)]
+                fac = [[None] * 8 for _ in range(8)]
+                inv = []
+                rows_l, rows_r = [], []
+                for t in range(8):
+                    d = row_of(cols[t], t)
+                    ri = lax.rsqrt(d)
+                    inv.append(ri)
+                    lt = cols[t] * ri
+                    for u in range(t + 1, 8):
+                        fac[t][u] = row_of(lt, u)
+                        cols[u] = cols[u] - lt * fac[t][u]
+                    pl_, pr_ = row_of(left, t), row_of(right, t)
+                    for k in range(t):
+                        pl_ = pl_ - fac[k][t] * rows_l[k]
+                        pr_ = pr_ - fac[k][t] * rows_r[k]
+                    rows_l.append(pl_ * ri)
+                    rows_r.append(pr_ * ri)
+                for h in range(g + 1, groups):
+                    hl, hr = panels[m][h]
+                    hc = [lane_of(hl, base + t) for t in range(8)]
+                    for t in range(8):
+                        ht = hc[t] * inv[t]
+                        for u in range(t + 1, 8):
+                            hc[u] = hc[u] - ht * fac[t][u]
+                        hl = hl - ht * rows_l[t]
+                        hr = hr - ht * rows_r[t]
+                    panels[m][h] = (hl, hr)
+                out_l, out_r = rows_l[0], rows_r[0]
+                for t in range(1, 8):
+                    out_l = jnp.where(sub == t, rows_l[t], out_l)
+                    out_r = jnp.where(sub == t, rows_r[t], out_r)
+                r[base:base + 8, :NB] = out_l
+                r[base:base + 8, NB:] = out_r
+        lo = SUB * (s + 1)
+        if lo < NB:
+            for r in refs:
+                got = r[SUB * s:lo, :]
+                r[lo:, :] = r[lo:, :] - dot(got[:, lo:NB], got, 0, 0)
+
+
+def chol_kernel(gu_ref, gi_ref, ru_ref, ri_ref, wu_ref, wi_ref, au, ai):
+    scale = F32(1.0)
+    row = lax.broadcasted_iota(jnp.int32, (NB, NB), 0)
+    col = lax.broadcasted_iota(jnp.int32, (NB, NB), 1)
+    eye = (row == col).astype(F32)
+    pairs = ((gu_ref, ru_ref, wu_ref, au), (gi_ref, ri_ref, wi_ref, ai))
+    for g, r, w, a in pairs:
+        r[...] = g[...]
+
+    def step(k, _):
+        at = pl.multiple_of(k * NB, NB)
+        for g, r, w, a in pairs:
+            a[:, :NB] = r[pl.ds(at, NB), pl.ds(at, NB)]
+            a[:, NB:] = eye
+        factor([p[3] for p in pairs])
+        for g, r, w, a in pairs:
+            w[pl.ds(at, NB), :] = a[:, NB:]
+            r[pl.ds(at, NB), pl.ds(at, NB)] = jnp.where(col >= row, a[:, :NB], 0.0)
+
+        def panel(j, _):
+            to = pl.multiple_of(j * NB, NB)
+            for g, r, w, a in pairs:
+                r[pl.ds(at, NB), pl.ds(to, NB)] = dot(a[:, NB:], r[pl.ds(at, NB), pl.ds(to, NB)], 1, 0)
+            return 0
+        lax.fori_loop(k + 1, KB, panel, 0)
+
+        def zero(j, _):
+            to = pl.multiple_of(j * NB, NB)
+            for g, r, w, a in pairs:
+                r[pl.ds(at, NB), pl.ds(to, NB)] = jnp.zeros((NB, NB), F32)
+            return 0
+        lax.fori_loop(0, k, zero, 0)
+
+        def outer(i, _):
+            ri = pl.multiple_of(i * NB, NB)
+
+            def inner(j, _):
+                to = pl.multiple_of(j * NB, NB)
+                for g, r, w, a in pairs:
+                    r[pl.ds(ri, NB), pl.ds(to, NB)] = r[pl.ds(ri, NB), pl.ds(to, NB)] - dot(r[pl.ds(at, NB), pl.ds(ri, NB)], r[pl.ds(at, NB), pl.ds(to, NB)], 0, 0)
+                return 0
+            lax.fori_loop(i, KB, inner, 0)
+            return 0
+        lax.fori_loop(k + 1, KB, outer, 0)
+        return 0
+
+    lax.fori_loop(0, KB, step, 0)
+
+
+def chol2(gu, gi):
+    full = jax.ShapeDtypeStruct((N, N), F32)
+    inv = jax.ShapeDtypeStruct((N, NB), F32)
+    vm = pl.BlockSpec(memory_space=pltpu.VMEM)
+    return pl.pallas_call(
+        chol_kernel,
+        out_shape=(full, full, inv, inv),
+        in_specs=[vm, vm],
+        out_specs=(vm, vm, vm, vm),
+        scratch_shapes=[pltpu.VMEM((NB, 2 * NB), F32)] * 2,
+        compiler_params=pltpu.CompilerParams(vmem_limit_bytes=48 << 20),
+        name="chol_pair",
+    )(gu, gi)
+
+
+def thin_kernel(e_ref, c_ref, ru_ref, ri_ref, wu_ref, wi_ref, out_ref, x, y):
+    x[...] = e_ref[...]
+    for k in range(KB - 1, -1, -1):
+        lo, hi = k * NB, (k + 1) * NB
+        xk = dot(x[:, lo:hi], wu_ref[lo:hi, :], 1, 0)
+        x[:, lo:hi] = xk
+        if k:
+            x[:, :lo] = x[:, :lo] - dot(xk, ru_ref[:lo, lo:hi], 1, 1)
+    y[...] = dot(x[...], c_ref[...], 1, 0)
+    for k in range(KB):
+        lo, hi = k * NB, (k + 1) * NB
+        yk = dot(y[:, lo:hi], wi_ref[lo:hi, :], 1, 1)
+        out_ref[:, lo:hi] = yk
+        if hi < N:
+            y[:, hi:] = y[:, hi:] - dot(yk, ri_ref[lo:hi, hi:], 1, 0)
+
+
+def thin(e, c, ru, ri, wu, wi):
+    vm = pl.BlockSpec(memory_space=pltpu.VMEM)
+    return pl.pallas_call(
+        thin_kernel,
+        out_shape=jax.ShapeDtypeStruct(e.shape, F32),
+        in_specs=[vm] * 6,
+        out_specs=vm,
+        scratch_shapes=[pltpu.VMEM(e.shape, F32)] * 2,
+        compiler_params=pltpu.CompilerParams(vmem_limit_bytes=48 << 20),
+        name="thin",
+    )(e, c, ru, ri, wu, wi)
 
 
 def body(user_table, item_table, pair_user, pair_item, pair_owner, pair_count):
@@ -32,13 +197,12 @@
     rows_out = width // devices
     root_total = jnp.sqrt(jnp.float32(total))
     gram_user, gram_item, cross = lax.psum((gram_user, gram_item, cross), ("pairs", "items"))
-    lower_user = jnp.linalg.cholesky(gram_user / total)
-    lower_item = jnp.linalg.cholesky(gram_item / total)
-    left = jax.scipy.linalg.solve_triangular(lower_user, cross / total, lower=True)
-    full = jax.scipy.linalg.solve_triangular(lower_item, left.T, lower=True).T * root_total
+    r_user, r_item, inv_user, inv_item = chol2(gram_user / total, gram_item / total)
     position = lax.axis_index(("pairs", "items"))
-    whitened = lax.dynamic_slice_in_dim(full, position * rows_out, rows_out, 0)
-    return (lower_user.T, lower_item.T, whitened)
+    rows = lax.broadcasted_iota(jnp.int32, (rows_out, width), 0) + position * rows_out
+    pick = (rows == lax.broadcasted_iota(jnp.int32, (rows_out, width), 1)).astype(F32)
+    whitened = thin(pick, cross / total, r_user, r_item, inv_user, inv_item) * root_total
+    return (r_user, r_item, whitened)
 
 
 def solution(mesh):

time: 1130 us -> 472 us (0.42)
  other arithmetic: 548 us -> 17.8 us
  matrix products: 153 us -> 28.8 us
  Pallas kernels: 0 us -> 91.5 us
  local copies, waits for them, and re-layouts: 135 us -> 58.9 us
    another operation x69 -> x2, other arithmetic: 519 us -> 1.32 us  [the longest x31 173 us: body(): lower_item = jnp.linalg.cholesky(gram_item / total)]
    another operation x58 -> x0, matrix products: 125 us -> none  [the longest x15 40 us: body(): jax.scipy.linalg.solve_triangular(lower_user, cross / total, lower=True)]
    pallas_call x0 -> x2, Pallas kernels: none -> 91.5 us  [the longest x1 78.2 us: chol2(): pl.pallas_call(chol_kernel, out_shape=(full, full, inv, inv), in_specs=[v...]
    another operation x68 -> x0, local copies, waits for them, and re-layouts: 51.3 us -> none  [the longest x24 23 us: body(): jax.scipy.linalg.solve_triangular(lower_user, cross / total, lower=True)]
    unnamed x21 -> x12, local copies, waits for them, and re-layouts: 15.7 us -> 1.76 us
  transfers between devices with their start and end apart: 2 -> 2, of which waited for: 2 -> 2; matrix products, arithmetic and copies ran while one was open for 2% -> 4% of each run, Pallas kernels for 0% -> 0%
where the time goes in v1:
time: 472 us; the launch traced here: 471 us
  waiting for transfers between devices  245 us (52%)
  Pallas kernels  91.5 us (19%)
  local copies, waits for them, and re-layouts  58.9 us (12%)
  matrix products  28.8 us (6%)
  other arithmetic  17.8 us (4%)
  between operations  14.8 us (3%)
  blocking collectives  8.84 us (2%)
  starting transfers between devices  5.83 us (1%)
    psum x1, waiting for transfers between devices, body(): lax.psum((gram_user, gram_item, cross), ('pairs', 'items'))  174 us
    pallas_call x1, Pallas kernels, chol2(): pl.pallas_call(chol_kernel, out_shape=(full, full, inv, inv), in_specs=[v...  78.2 us
    all_to_all x1, waiting for transfers between devices, body(): lax.all_to_all(rows, 'items', split_axis=0, concat_axis=0, tiled=True)  70.8 us
    gather x1, local copies, waits for them, and re-layouts, body(): rows = jnp.take(item_table, wanted.reshape(-1), axis=0)  23.6 us
    gather x1, local copies, waits for them, and re-layouts, body(): jnp.take(fetched.reshape(owners * capacity, width), flat_slot, axis=0)  15.5 us
    pallas_call x1, Pallas kernels, thin(): pl.pallas_call(thin_kernel, out_shape=jax.ShapeDtypeStruct(e.shape, F32),...  13.3 us
    dot_general x1, matrix products, body(): lax.dot_general(user_panel, item_panel, dims, preferred_element_type=jnp....  10.7 us
    dot_general x1, matrix products, body(): lax.dot_general(user_panel, user_panel, dims, preferred_element_type=jnp....  10.7 us
  transfers between devices with their start and end apart: 2, of which 2 were waited for; matrix products, arithmetic and copies ran while one was open for 4% of the time, Pallas kernels for 0%

profile of v1, /device:TPU:1, one launch (start us, length us, event | category | flops | bytes accessed | tf_op | source)
XLA Modules:
  0.0 471.1 jit_solution(9644986294214451353)
XLA Ops:
  7.2 0.0 copy-start
  7.2 0.9 fusion.2
  8.0 1.1 reduce-window.6
  9.2 0.2 slice_reduce_fusion
  9.4 0.2 reduce-window.9
  9.6 0.1 add_bitcast_fusion
  9.7 0.7 fusion.1
  10.4 0.7 compare_and_fusion.1
  11.1 8.2 %scatter_custom_fusion = s32[4096]{0:T(1024)S(1)} fusion(s32[2048]{0:T(1024)S(1)} %get-tuple-element.15, s32[2048]{0:T(1024)} %param.9, s32[]{:T(128)} %constant.41.clone.1), kind=kCustom, calls=%fused_computation.27 | custom fusion | bytes 16896 | tf_op jit(solution)/shard_map/scatter | solution.py:182
  19.3 8.8 %all_to_all.14 = s32[4,1,1024]{2,1,0:T(1,128)S(1)} all-to-all(s32[4,1,1024]{2,1,0:T(1,128)S(1)} %bitcast.30), channel_id=1, replica_groups=mesh['pairs'=32,'items'=4] {'items'}, dimensions={0} | all-to-all | bytes 32768 | tf_op jit(solution)/shard_map/all_to_all | solution.py:184
  28.2 23.6 %gather_fusion.1 = bf16[4096,1024]{1,0:T(8,128)(2,1)} fusion(bf16[2048,1024]{1,0:T(8,128)(2,1)} %param.7, s32[4096]{0:T(1024)S(1)} %broadcast_clamp_fusion), kind=kCustom, calls=%fused_computation.1 | custom fusion | bytes 16793600 | tf_op jit(solution)/shard_map/jit(_take)/gather | solution.py:185
  51.9 7.3 %broadcast_select_fusion = bf16[4,1024,1024]{2,1,0:T(8,128)(2,1)} fusion(bf16[4,1024,1024]{2,1,0:T(8,128)(2,1)} %bitcast.27, pred[4,1024]{1,0:T(4,128)(4,1)S(1)} %compare_and_fusion), kind=kLoop, calls=%fused_computation.4 | loop fusion | flops 4194304 | bytes 16781312 | tf_op jit(solution)/shard_map/jit(_take)/select_n | solution.py:185
  59.1 5.8 %all-to-all-start.1 = ((bf16[4,1024,1024]{2,1,0:T(8,128)(2,1)}), bf16[4,1024,1024]{2,1,0:T(8,128)(2,1)}, u32[]{:S(2)}, u32[]{:S(2)}) async-start(bf16[4,1024,1024]{2,1,0:T(8,128)(2,1)} %broadcast_select_fusion), calls=%async_computation.1 | async-start | bytes 16777216 | tf_op jit(solution)/shard_map/all_to_all | solution.py:187
  64.9 0.0 all-reduce.3.cloned.1.call-start
  65.6 0.0 copy-done.5
  65.7 0.0 copy-done
  65.7 9.6 %gather_fusion = bf16[2048,1024]{1,0:T(8,128)(2,1)} fusion(bf16[1024,1024]{1,0:T(8,128)(2,1)S(1)} %copy-done, s32[2048]{0:T(1024)S(1)} %fusion.6), kind=kCustom, calls=%fused_computation | custom fusion | bytes 8396800 | tf_op jit(solution)/shard_map/jit(_take)/gather | solution.py:190
  75.3 10.7 %fusion.8 = f32[1024,1024]{1,0:T(8,128)} fusion(bf16[2048,1024]{1,0:T(8,128)(2,1)} %gather_fusion, pred[2048]{0:T(1024)(128)(4,1)S(1)} %get-tuple-element.17, pred[2048]{0:T(1024)(128)(4,1)S(1)} %get-tuple-element.16), kind=kOutput, calls=%fused_computation.36 | convolution fusion | flops 4299161600 | bytes 8392704 | tf_op jit(solution)/shard_map/dot_general | solution.py:194
  86.0 70.8 %all-to-all-done.1 = bf16[4,1024,1024]{2,1,0:T(8,128)(2,1)} async-done(((bf16[4,1024,1024]{2,1,0:T(8,128)(2,1)}), bf16[4,1024,1024]{2,1,0:T(8,128)(2,1)}, u32[]{:S(2)}, u32[]{:S(2)}) %all-to-all-start.1) | async-done | bytes 8388640 | tf_op jit(solution)/shard_map/all_to_all | solution.py:187
  156.7 15.5 %gather_fusion.2 = bf16[2048,1024]{1,0:T(8,128)(2,1)} fusion(bf16[4096,1024]{1,0:T(8,128)(2,1)} %bitcast.7, s32[2048]{0:T(1024)S(1)} %broadcast_clamp_fusion.1), kind=kCustom, calls=%fused_computation.2 | custom fusion | bytes 8396800 | tf_op jit(solution)/shard_map/jit(_take)/gather | solution.py:188
  172.2 10.7 %fusion.7 = f32[1024,1024]{1,0:T(8,128)} fusion(bf16[2048,1024]{1,0:T(8,128)(2,1)} %gather_fusion, pred[2048]{0:T(1024)(128)(4,1)S(1)} %get-tuple-element.17, pred[2048]{0:T(1024)(128)(4,1)S(1)} %get-tuple-element.16, bf16[2048,1024]{1,0:T(8,128)(2,1)} %gather_fusion.2, pred[2048]{0:T(1024)(128)(4,1)S(1)} %get-tuple-element.14), kind=kOutput, calls=%fused_computation.35 | convolution fusion | flops 4303355904 | bytes 12589056 | tf_op jit(solution)/shard_map/dot_general | solution.py:196
  183.0 7.4 %fusion.9 = f32[1024,1024]{1,0:T(8,128)} fusion(bf16[2048,1024]{1,0:T(8,128)(2,1)S(1)} %copy-done.2, pred[2048]{0:T(1024)(128)(4,1)S(1)} %get-tuple-element.14, pred[2048]{0:T(1024)(128)(4,1)S(1)} %get-tuple-element.16), kind=kOutput, calls=%fused_computation.37 | convolution fusion | flops 4299161600 | bytes 8392704 | tf_op jit(solution)/shard_map/dot_general | solution.py:195
  190.3 0.0 all-reduce.3.cloned.1.call-update
  190.4 0.1 fusion.3.e_ref
  190.5 173.8 %all-reduce.3.cloned.1.call-done = (f32[1024,1024]{1,0:T(8,128)}, f32[1024,1024]{1,0:T(8,128)}, f32[1024,1024]{1,0:T(8,128)}) async-done(((f32[1024,1024]{1,0:T(8,128)}, f32[1024,1024]{1,0:T(8,128)}, f32[1024,1024]{1,0:T(8,128)}), (f32[1024,1024]{1,0:T(8,128)}, f32[1024,1024]{1,0:T(8,128)}, f32[1024,1024]{1,0:T(8,128)})) %all-reduce.3.cloned.1.call-update) | async-done | bytes 12582928 | tf_op jit(solution)/shard_map/psum | solution.py:199
  364.3 5.1 %broadcast_multiply_fusion.1.gi_ref = f32[1024,1024]{1,0:T(8,128)} fusion(f32[1024,1024]{1,0:T(8,128)} %get-tuple-element.12), kind=kLoop, calls=%fused_computation.8 | loop fusion | flops 1048576 | bytes 8388608 | tf_op jit(solution)/shard_map/div | solution.py:200
  369.4 0.4 broadcast_multiply_fusion.2.gu_ref
  369.9 1.7 copy-done.3
  371.6 0.4 broadcast_multiply_fusion.c_ref
  372.0 78.2 %chol_pair.1 = (f32[1024,1024]{1,0:T(8,128)}, f32[1024,1024]{1,0:T(8,128)}, f32[1024,128]{1,0:T(8,128)S(1)}, f32[1024,128]{1,0:T(8,128)S(1)}) custom-call(f32[1024,1024]{1,0:T(8,128)S(1)} %broadcast_multiply_fusion.2.gu_ref, f32[1024,1024]{1,0:T(8,128)} %broadcast_multiply_fusion.1.gi_ref), custom_call_target="tpu_custom_call" | custom-call | tf_op jit(solution)/shard_map/chol_pair/pallas_call | solution.py:131
  450.3 13.3 %thin.1 = f32[8,1024]{1,0:T(8,128)S(1)} custom-call(f32[8,1024]{1,0:T(8,128)S(1)} %fusion.3.e_ref, f32[1024,1024]{1,0:T(8,128)S(1)} %broadcast_multiply_fusion.c_ref, f32[1024,1024]{1,0:T(8,128)} %get-tuple-element.4.ru_ref, f32[1024,1024]{1,0:T(8,128)} %get-tuple-element.5.ri_ref, f32[1024,128]{1,0:T(8,128)S(1)} %get-tuple-element.9.wu_ref, ...), custom_call_target="tpu_custom_call" | custom-call | tf_op jit(solution)/shard_map/thin/pallas_call | solution.py:161
  463.6 0.7 broadcast_multiply_fusion.3
  (15 shorter events, 0.1 us)
Async XLA Ops:
  7.2 58.5 %copy-start = (bf16[1024,1024]{1,0:T(8,128)(2,1)S(1)}, bf16[1024,1024]{1,0:T(8,128)(2,1)}, u32[]{:S(2)}) copy-start(bf16[1024,1024]{1,0:T(8,128)(2,1)} %param.6) | copy-start | bytes 6291460
  59.1 6.5 %copy-start.5 = (s32[2048]{0:T(1024)S(1)}, s32[2048]{0:T(1024)}, u32[]{:S(2)}) copy-start(s32[2048]{0:T(1024)} %param.8) | copy-start | bytes 24580
  59.1 97.6 %all-to-all-start.1 = ((bf16[4,1024,1024]{2,1,0:T(8,128)(2,1)}), bf16[4,1024,1024]{2,1,0:T(8,128)(2,1)}, u32[]{:S(2)}, u32[]{:S(2)}) async-start(bf16[4,1024,1024]{2,1,0:T(8,128)(2,1)} %broadcast_select_fusion), calls=%async_computation.1 | async-start | bytes 16777216 | tf_op jit(solution)/shard_map/all_to_all | solution.py:187
  64.9 299.3 %all-reduce.3.cloned.1.call-start = ((), (), s32[]{:S(2)}) async-start(), calls=%async_computation.2 | async-start | bytes 25165824 | tf_op jit(solution)/shard_map/psum | solution.py:199
  172.2 10.7 %copy-start.2 = (bf16[2048,1024]{1,0:T(8,128)(2,1)S(1)}, bf16[2048,1024]{1,0:T(8,128)(2,1)}, u32[]{:S(2)}) copy-start(bf16[2048,1024]{1,0:T(8,128)(2,1)} %gather_fusion.2) | copy-start | bytes 12582916
  364.3 5.1 %copy-start.4 = (f32[1024,1024]{1,0:T(8,128)S(1)}, f32[1024,1024]{1,0:T(8,128)}, u32[]{:S(2)}) copy-start(f32[1024,1024]{1,0:T(8,128)} %get-tuple-element.11) | copy-start | bytes 12582916
  369.4 2.2 copy-start.3
  450.3 13.9 %copy-start.1 = (bf16[1024,1024]{1,0:T(8,128)(2,1)S(1)}, bf16[1024,1024]{1,0:T(8,128)(2,1)}, u32[]{:S(2)}) copy-start(bf16[1024,1024]{1,0:T(8,128)(2,1)} %param.6) | copy-start | bytes 6291460
Sparse Core Ops, SparseCore 0:
  190.5 173.7 all-reduce.2
